TPU v7x, 128 devices: a whole 4x4x4 slice. The times are simulated.
128 devices in a mesh: row: 8 (over y, core), col: 16 (over z, x).
Axes of the slice: x: 4, y: 4, z: 4, core: 2. Of those that a mesh axis runs over, the one named last changes fastest.
Arguments:
- tokens_in: bfloat16 [1024, 16384], P('row', 'col'), may hold values from -6 to 6
- out_grads: bfloat16 [1024, 16384], P('col', 'row'), may hold values from -0.1875 to 0.1875
- loc_rows: int32 [2048], replicated, may hold values from 0 to 16383
- loc_cols: int32 [2048], replicated, may hold values from 0 to 16383
Outputs:
- coef_grads: float32 [2048], P('col')
All inputs are finite; a program needn't handle non-finite values.
Results may differ from a plain program's by a relative error of at most 0.0003.
Values may be sent and summed in bfloat16 or wider, within the bound.
A program may use at most 64 MiB of HBM per device.

v0:
```python
import math

import jax
import jax.numpy as jnp
import numpy as np
from jax import lax
from jax.experimental import pallas as pl
from jax.experimental.pallas import tpu as pltpu
from jax.sharding import PartitionSpec as P

N = 16384
HALF = 128
FP = 136
TOK = 8
MESH = pl.DeviceIdType.MESH
F32, BF16 = jnp.float32, jnp.bfloat16


def halves(table):
    high = table.astype(np.float32).astype(BF16)
    low = (table - high.astype(np.float64)).astype(np.float32).astype(BF16)
    return high, low


def tables():
    slot = np.arange(FP)[:, None]
    valid = (slot <= HALF).astype(np.float64)
    h = np.arange(HALF)[None, :]
    turn = 2 * np.pi * ((h * slot) % 256) / 256
    over_h = np.concatenate([np.cos(turn) * valid, np.sin(turn) * valid])
    high, low = halves(over_h)
    first = np.concatenate([high, low], axis=1)
    odd = 2 * h + 1
    turn = np.pi * (odd * slot) / (2 * N)
    twiddle = np.stack([np.cos(turn), np.sin(turn)]).astype(np.float32)
    g = np.concatenate([np.arange(64), np.arange(1, 65)])[None, :]
    sign = np.concatenate([-np.ones(64), np.ones(64)])[None, :]
    turn = np.pi * ((odd.T * g) % 256) / HALF
    over_l = np.concatenate([np.cos(turn), sign * np.sin(turn)])
    high, low = halves(over_l)
    second = np.concatenate([high, low], axis=1)
    return first, twiddle, second


def digits(loc):
    rest = loc & 255
    mirrored = rest > HALF
    slot = jnp.where(mirrored, 256 - rest, rest)
    column = (loc >> 8) + jnp.where(mirrored, 64, 0)
    return slot, column


def kernel(nr, nc, x_hbm, g_hbm, rows_hbm, cols_hbm, first_hbm, twiddle_hbm, second_hbm, o_ref,
           x_in, g_in, rows, cols, first, twiddle, second, spread, packed, z_high, z_low, d_pair,
           pick, picked, part, got_col, sent_row, got_row,
           local_sem, x_send, x_recv, g_send, g_recv, c_send, c_recv, r_send, r_recv):
    r, c = lax.axis_index("row"), lax.axis_index("col")
    locs = rows.shape[1]

    def x_dest(j):
        return lax.rem(j, nr), 2 * r + lax.div(j, nr)

    def is_me(row, col):
        return jnp.logical_and(row == r, col == c)

    barrier = pltpu.get_barrier_semaphore()

    def greet(row, col):
        pl.semaphore_signal(barrier, inc=1, device_id=(row, col), device_id_type=MESH)

    for i in range(1, nr):
        greet(lax.rem(r + i, nr), c)
    for i in range(1, nc):
        greet(r, lax.rem(c + i, nc))
    for i in range(nc):
        source = lax.rem(c + i, nc)

        @pl.when(jnp.logical_not(is_me(lax.div(c, 2), source)))
        def _():
            greet(lax.div(c, 2), source)

    loads = [(rows_hbm, rows), (cols_hbm, cols), (first_hbm, first), (twiddle_hbm, twiddle), (second_hbm, second)]
    loads = [pltpu.make_async_copy(a, b, local_sem.at[i]) for i, (a, b) in enumerate(loads)]
    for load in loads:
        load.start()

    kept = jnp.logical_and(c >= 2 * r, c < 2 * r + 2).astype(jnp.int32)
    pl.semaphore_wait(barrier, (nr - 1) + (nc - 1) + nc - kept)

    def g_copy(i):
        s = lax.rem(r + i, nr)
        return pltpu.make_async_remote_copy(
            src_ref=g_hbm.at[s], dst_ref=g_in.at[r], send_sem=g_send.at[i], recv_sem=g_recv.at[r],
            device_id=(s, c), device_id_type=MESH)

    def x_copy(i):
        j = lax.rem(c + i, nc)
        return pltpu.make_async_remote_copy(
            src_ref=x_hbm.at[j], dst_ref=x_in.at[c], send_sem=x_send.at[i], recv_sem=x_recv.at[c],
            device_id=x_dest(j), device_id_type=MESH)

    def x_stays(i):
        return is_me(*x_dest(lax.rem(c + i, nc)))

    def x_local(i):
        return pltpu.make_async_copy(x_hbm.at[lax.rem(c + i, nc)], x_in.at[c], x_recv.at[c])

    pltpu.make_async_copy(g_hbm.at[r], g_in.at[r], g_recv.at[r]).start()
    for i in range(1, nr):
        g_copy(i).start()
    for i in range(nc):
        @pl.when(x_stays(i))
        def _():
            x_local(i).start()

        @pl.when(jnp.logical_not(x_stays(i)))
        def _():
            x_copy(i).start()

    for load in loads:
        load.wait()

    for side, loc_ref in ((0, rows), (1, cols)):
        _, column = digits(loc_ref[...])
        lane = lax.broadcasted_iota(jnp.int32, (HALF, locs), 0)
        hot = (lane == column).astype(F32).astype(BF16)
        pick[side, :HALF, :] = hot
        pick[side, HALF:, :] = hot

    def spectrum(side, arrived, recv_sem, loc_ref):
        sources, _, width = arrived.shape
        steps = width // HALF
        for s in range(sources):
            pltpu.make_async_copy(arrived.at[s], arrived.at[s], recv_sem.at[s]).wait()
            block = arrived[s].astype(F32)
            for k in range(steps):
                spread[pl.ds((s * steps + k) * TOK, TOK), :] = block[:, k * HALF:(k + 1) * HALF]
        for t in range(TOK):
            column = spread[pl.ds(t, HALF, stride=TOK), :].astype(BF16)
            packed[:HALF, t * HALF:(t + 1) * HALF] = column
            packed[HALF:, t * HALF:(t + 1) * HALF] = column
        tc, ts = twiddle[0], twiddle[1]
        for t in range(TOK):
            if t % 2 == 0:
                both = jnp.dot(first[...], packed[:, t * HALF:(t + 2) * HALF], preferred_element_type=F32)
            y = both[:, (t % 2) * HALF:(t % 2 + 1) * HALF]
            yc, ys = y[:FP], y[FP:]
            for part_at, z in ((0, yc * tc - ys * ts), (HALF, yc * ts + ys * tc)):
                high = z.astype(BF16)
                z_high[t * FP:(t + 1) * FP, part_at:part_at + HALF] = high
                z_low[t * FP:(t + 1) * FP, part_at:part_at + HALF] = (z - high.astype(F32)).astype(BF16)
        wide = jnp.dot(z_high[...], second[...], preferred_element_type=F32)
        d = wide[:, :HALF] + wide[:, HALF:] + jnp.dot(z_low[...], second[:, :HALF], preferred_element_type=F32)
        high = d.astype(BF16)
        d_pair[:, :HALF] = high
        d_pair[:, HALF:] = (d - high.astype(F32)).astype(BF16)
        tile = 256
        for k in range(locs // tile):
            at = slice(k * tile, (k + 1) * tile)
            slot, _ = digits(loc_ref[:, at])
            found = jnp.dot(d_pair[...], pick[side, :, at], preferred_element_type=F32)
            mask = lax.broadcasted_iota(jnp.int32, (FP, tile), 0) == slot
            for t in range(TOK):
                mine = jnp.where(mask, found[t * FP:(t + 1) * FP], 0.0)
                picked[side, t:t + 1, at] = jnp.sum(mine, axis=0, keepdims=True)

    spectrum(0, g_in, g_recv, rows)
    spectrum(1, x_in, x_recv, cols)

    def norming(loc_ref):
        return jnp.where(loc_ref[...] == 0, math.sqrt(1.0 / N), math.sqrt(2.0 / N))

    total = jnp.sum(picked[0] * picked[1], axis=0, keepdims=True) * (norming(rows) * norming(cols))
    width = locs // nc
    for k in range(nc):
        part[k] = total[:, k * width:(k + 1) * width]

    got_col[c] = part[c]

    def col_copy(i):
        d = lax.rem(c + i, nc)
        return pltpu.make_async_remote_copy(
            src_ref=part.at[d], dst_ref=got_col.at[c], send_sem=c_send.at[i], recv_sem=c_recv.at[c],
            device_id=(r, d), device_id_type=MESH)

    for i in range(1, nc):
        col_copy(i).start()
    for i in range(1, nc):
        d = lax.rem(c + i, nc)
        pltpu.make_async_copy(got_col.at[d], got_col.at[d], c_recv.at[d]).wait()
    mine = got_col[0]
    for k in range(1, nc):
        mine = mine + got_col[k]
    sent_row[...] = mine
    got_row[r] = mine

    def row_copy(i):
        d = lax.rem(r + i, nr)
        return pltpu.make_async_remote_copy(
            src_ref=sent_row, dst_ref=got_row.at[r], send_sem=r_send.at[i], recv_sem=r_recv.at[r],
            device_id=(d, c), device_id_type=MESH)

    for i in range(1, nr):
        row_copy(i).start()
    for i in range(1, nr):
        d = lax.rem(r + i, nr)
        pltpu.make_async_copy(got_row.at[d], got_row.at[d], r_recv.at[d]).wait()
    result = got_row[0]
    for k in range(1, nr):
        result = result + got_row[k]
    o_ref[...] = result

    for i in range(1, nr):
        g_copy(i).wait_send()
        row_copy(i).wait_send()
    for i in range(1, nc):
        col_copy(i).wait_send()
    for i in range(nc):
        @pl.when(jnp.logical_not(x_stays(i)))
        def _():
            x_copy(i).wait_send()


def solution(mesh):
    nr, nc = mesh.shape["row"], mesh.shape["col"]
    first, twiddle, second = tables()

    def local(tokens_in, out_grads, loc_rows, loc_cols):
        locs = loc_rows.shape[0]
        x = tokens_in.reshape(nc, TOK, tokens_in.shape[1])
        g = out_grads.reshape(nr, TOK, out_grads.shape[1])
        width = locs // nc
        dma = pltpu.SemaphoreType.DMA
        out = pl.pallas_call(
            lambda *refs: kernel(nr, nc, *refs),
            out_shape=jax.ShapeDtypeStruct((1, width), F32),
            in_specs=[pl.BlockSpec(memory_space=pl.ANY)] * 7,
            out_specs=pl.BlockSpec(memory_space=pltpu.VMEM),
            scratch_shapes=[
                pltpu.VMEM((nc, TOK, x.shape[2]), BF16),
                pltpu.VMEM((nr, TOK, g.shape[2]), BF16),
                pltpu.VMEM((1, locs), jnp.int32),
                pltpu.VMEM((1, locs), jnp.int32),
                pltpu.VMEM(first.shape, BF16),
                pltpu.VMEM(twiddle.shape, F32),
                pltpu.VMEM(second.shape, BF16),
                pltpu.VMEM((HALF * TOK, HALF), F32),
                pltpu.VMEM((2 * HALF, TOK * HALF), BF16),
                pltpu.VMEM((TOK * FP, 2 * HALF), BF16),
                pltpu.VMEM((TOK * FP, 2 * HALF), BF16),
                pltpu.VMEM((TOK * FP, 2 * HALF), BF16),
                pltpu.VMEM((2, 2 * HALF, locs), BF16),
                pltpu.VMEM((2, TOK, locs), F32),
                pltpu.VMEM((nc, 1, width), F32),
                pltpu.VMEM((nc, 1, width), F32),
                pltpu.VMEM((1, width), F32),
                pltpu.VMEM((nr, 1, width), F32),
                dma((5,)), dma((nc,)), dma((nc,)), dma((nr,)), dma((nr,)),
                dma((nc,)), dma((nc,)), dma((nr,)), dma((nr,)),
            ],
            compiler_params=pltpu.CompilerParams(collective_id=0, has_side_effects=True, vmem_limit_bytes=48 << 20),
            name="spectral",
        )(x, g, loc_rows.reshape(1, locs), loc_cols.reshape(1, locs),
          jnp.asarray(first), jnp.asarray(twiddle), jnp.asarray(second))
        return out.reshape(width)

    in_specs = (P("row", "col"), P("col", "row"), P(), P())
    return jax.shard_map(local, mesh=mesh, in_specs=in_specs, out_specs=P("col"), check_vma=False)
```

profile of v0, /device:TPU:1, one launch (start us, length us, event | category | flops | bytes accessed | tf_op | source)
XLA Modules:
  0.0 35.5 jit_solution(7526025507173960377)
XLA Ops:
  0.0 0.0 copy-start
  0.0 0.9 %copy-done = bf16[128,1024]{1,0:T(8,128)(2,1)S(1)} copy-done((bf16[128,1024]{1,0:T(8,128)(2,1)S(1)}, bf16[128,1024]{1,0:T(8,128)(2,1)}, u32[]{:S(2)}) %copy-start) | copy-done | bytes 262168
  1.0 0.0 copy-start.1
  1.0 0.9 %copy-done.1 = bf16[64,2048]{1,0:T(8,128)(2,1)S(1)} copy-done((bf16[64,2048]{1,0:T(8,128)(2,1)S(1)}, bf16[64,2048]{1,0:T(8,128)(2,1)}, u32[]{:S(2)}) %copy-start.1) | copy-done | bytes 262168
  1.9 0.0 copy-start.2
  1.9 0.9 %copy-done.2 = f32[2,136,128]{2,1,0:T(8,128)S(1)} copy-done((f32[2,136,128]{2,1,0:T(8,128)S(1)}, f32[2,136,128]{2,1,0:T(8,128)}, u32[]{:S(2)}) %copy-start.2) | copy-done | bytes 139288
  2.8 0.0 copy-start.3
  2.8 0.9 %copy-done.3 = bf16[272,256]{1,0:T(8,128)(2,1)S(1)} copy-done((bf16[272,256]{1,0:T(8,128)(2,1)S(1)}, bf16[272,256]{1,0:T(8,128)(2,1)}, u32[]{:S(2)}) %copy-start.3) | copy-done | bytes 139288
  3.7 0.0 copy-start.4
  3.7 0.9 %copy-done.4 = bf16[256,256]{1,0:T(8,128)(2,1)S(1)} copy-done((bf16[256,256]{1,0:T(8,128)(2,1)S(1)}, bf16[256,256]{1,0:T(8,128)(2,1)}, u32[]{:S(2)}) %copy-start.4) | copy-done | bytes 131096
  4.6 0.0 copy-start.5
  4.6 0.7 %copy-done.5 = s32[2048]{0:T(1024)S(1)} copy-done((s32[2048]{0:T(1024)S(1)}, s32[2048]{0:T(1024)}, u32[]{:S(2)}) %copy-start.5) | copy-done | bytes 8216
  5.3 0.0 copy-start.6
  5.3 0.7 %copy-done.6 = s32[2048]{0:T(1024)S(1)} copy-done((s32[2048]{0:T(1024)S(1)}, s32[2048]{0:T(1024)}, u32[]{:S(2)}) %copy-start.6) | copy-done | bytes 8216
  6.0 28.9 %spectral.1 = f32[1,128]{1,0:T(1,128)S(1)} custom-call(bf16[16,8,1024]{2,1,0:T(8,128)(2,1)S(1)} %bitcast.5, bf16[8,8,2048]{2,1,0:T(8,128)(2,1)S(1)} %bitcast.6, s32[1,2048]{1,0:T(1,128)S(1)} %bitcast.7, s32[1,2048]{1,0:T(1,128)S(1)} %bitcast.8, bf16[272,256]{1,0:T(8,128)(2,1)S(1)} %copy-done.3, f32[2,136,128]{2,1,0:T(8,128)S(1)} %copy-done.2, ...), custom_call_target="tpu_custom_call" | custom-call | tf_op jit(solution)/shard_map/spectral/pallas_call | solution.py:234
  34.9 0.5 %copy.9 = f32[128]{0:T(128)} copy(f32[128]{0:T(128)S(1)} %bitcast.9) | data formatting | bytes 1024
Async XLA Ops:
  0.0 0.9 %copy-start = (bf16[128,1024]{1,0:T(8,128)(2,1)S(1)}, bf16[128,1024]{1,0:T(8,128)(2,1)}, u32[]{:S(2)}) copy-start(bf16[128,1024]{1,0:T(8,128)(2,1)} %param.7) | copy-start | bytes 786436
  1.0 0.9 %copy-start.1 = (bf16[64,2048]{1,0:T(8,128)(2,1)S(1)}, bf16[64,2048]{1,0:T(8,128)(2,1)}, u32[]{:S(2)}) copy-start(bf16[64,2048]{1,0:T(8,128)(2,1)} %param.8) | copy-start | bytes 786436
  1.9 0.9 %copy-start.2 = (f32[2,136,128]{2,1,0:T(8,128)S(1)}, f32[2,136,128]{2,1,0:T(8,128)}, u32[]{:S(2)}) copy-start(f32[2,136,128]{2,1,0:T(8,128)} %constant.7.clone.refs_5_) | copy-start | bytes 417796
  2.8 0.9 %copy-start.3 = (bf16[272,256]{1,0:T(8,128)(2,1)S(1)}, bf16[272,256]{1,0:T(8,128)(2,1)}, u32[]{:S(2)}) copy-start(bf16[272,256]{1,0:T(8,128)(2,1)} %constant.6.clone.refs_4_) | copy-start | bytes 417796
  3.7 0.9 %copy-start.4 = (bf16[256,256]{1,0:T(8,128)(2,1)S(1)}, bf16[256,256]{1,0:T(8,128)(2,1)}, u32[]{:S(2)}) copy-start(bf16[256,256]{1,0:T(8,128)(2,1)} %constant.8.clone.refs_6_) | copy-start | bytes 393220
  4.6 0.7 %copy-start.5 = (s32[2048]{0:T(1024)S(1)}, s32[2048]{0:T(1024)}, u32[]{:S(2)}) copy-start(s32[2048]{0:T(1024)} %param.9) | copy-start | bytes 24580
  5.3 0.7 %copy-start.6 = (s32[2048]{0:T(1024)S(1)}, s32[2048]{0:T(1024)}, u32[]{:S(2)}) copy-start(s32[2048]{0:T(1024)} %param.10) | copy-start | bytes 24580
where the time goes:
time: 35.8 us; the launch traced here: 35.5 us
  Pallas kernels  28.9 us (81%)
  local copies, waits for them, and re-layouts  6.52 us (18%)
    pallas_call x1, Pallas kernels, local(): pl.pallas_call(lambda *refs: kernel(nr, nc, *refs), out_shape=jax.ShapeDt...  28.9 us
    unnamed x15, local copies, waits for them, and re-layouts  6.52 us

commit v1 on v0

--- a/solution.py
+++ b/solution.py
@@ -52,70 +52,112 @@
 
 def kernel(nr, nc, x_hbm, g_hbm, rows_hbm, cols_hbm, first_hbm, twiddle_hbm, second_hbm, o_ref,
            x_in, g_in, rows, cols, first, twiddle, second, spread, packed, z_high, z_low, d_pair,
-           pick, picked, part, got_col, sent_row, got_row,
-           local_sem, x_send, x_recv, g_send, g_recv, c_send, c_recv, r_send, r_recv):
+           pick, picked, part, got,
+           load_sem, x_send, x_recv, g_send, g_recv, p_send, p_recv, x_ready, g_ready, peers, everyone):
     r, c = lax.axis_index("row"), lax.axis_index("col")
+    y, core, z, x = r // 2, r % 2, c // 4, c % 4
     locs = rows.shape[1]
 
+    def row_place(row):
+        return (4 * (row // 2) - 2 * (row % 2)) * nr * nc + row
+
+    def col_place(col):
+        return (6 * (col // 4) + 5 * (col % 4) - 7 * (col % 4 // 3)) * nr * nc + col * nr
+
+    def place_of(device):
+        return row_place(device[0]) + col_place(device[1])
+
+    place = place_of((r, c))
+
+    x_row = 2 * z + x // 2
+    my_g = 2 * ((y - z + 4) % 4) + core
+    my_x = nr * (x % 2) + my_g
+
     def x_dest(j):
-        return lax.rem(j, nr), 2 * r + lax.div(j, nr)
-
-    def is_me(row, col):
-        return jnp.logical_and(row == r, col == c)
+        return 2 * ((y + j // 2) % 4) + j % 2, 4 * y + 2 * core + j // nr
+
+    def g_dest(s):
+        return 2 * ((z + s // 2) % 4) + s % 2, c
+
+    def signal(sem, device):
+        pl.semaphore_signal(sem, inc=1, device_id=device, device_id_type=MESH)
 
     barrier = pltpu.get_barrier_semaphore()
-
-    def greet(row, col):
-        pl.semaphore_signal(barrier, inc=1, device_id=(row, col), device_id_type=MESH)
-
-    for i in range(1, nr):
-        greet(lax.rem(r + i, nr), c)
-    for i in range(1, nc):
-        greet(r, lax.rem(c + i, nc))
-    for i in range(nc):
-        source = lax.rem(c + i, nc)
-
-        @pl.when(jnp.logical_not(is_me(lax.div(c, 2), source)))
-        def _():
-            greet(lax.div(c, 2), source)
+    partners = [x_dest(j) for j in range(nc)] + [(x_row, j) for j in range(nc)] + [(r, j) for j in range(nc)]
+    partners += [(s, c) for s in range(nr)]
+    count = 0
+    for device in partners:
+        there = place_of(device)
+
+        @pl.when(there > place)
+        def _():
+            signal(barrier, device)
+
+        count = count + (there < place).astype(jnp.int32)
 
     loads = [(rows_hbm, rows), (cols_hbm, cols), (first_hbm, first), (twiddle_hbm, twiddle), (second_hbm, second)]
-    loads = [pltpu.make_async_copy(a, b, local_sem.at[i]) for i, (a, b) in enumerate(loads)]
+    loads = [pltpu.make_async_copy(a, b, load_sem.at[i]) for i, (a, b) in enumerate(loads)]
     for load in loads:
         load.start()
 
-    kept = jnp.logical_and(c >= 2 * r, c < 2 * r + 2).astype(jnp.int32)
-    pl.semaphore_wait(barrier, (nr - 1) + (nc - 1) + nc - kept)
+    def wait_for(sem, number):
+        @pl.when(number > 0)
+        def _():
+            pl.semaphore_wait(sem, number)
+
+    wait_for(barrier, count)
+
+    def tell_earlier(sem, device):
+        @pl.when(place_of(device) < place)
+        def _():
+            signal(sem, device)
 
     def g_copy(i):
-        s = lax.rem(r + i, nr)
+        s = (r + i) % nr
+        return s, g_dest(s), g_hbm.at[s], g_in.at[r], g_send, g_recv.at[y]
+
+    def x_copy(i):
+        j = (c + i) % nc
+        return j, x_dest(j), x_hbm.at[j], x_in.at[c], x_send, x_recv.at[z]
+
+    def remote(device, src, dst, send_sem, recv_sem):
         return pltpu.make_async_remote_copy(
-            src_ref=g_hbm.at[s], dst_ref=g_in.at[r], send_sem=g_send.at[i], recv_sem=g_recv.at[r],
-            device_id=(s, c), device_id_type=MESH)
-
-    def x_copy(i):
-        j = lax.rem(c + i, nc)
-        return pltpu.make_async_remote_copy(
-            src_ref=x_hbm.at[j], dst_ref=x_in.at[c], send_sem=x_send.at[i], recv_sem=x_recv.at[c],
-            device_id=x_dest(j), device_id_type=MESH)
-
-    def x_stays(i):
-        return is_me(*x_dest(lax.rem(c + i, nc)))
-
-    def x_local(i):
-        return pltpu.make_async_copy(x_hbm.at[lax.rem(c + i, nc)], x_in.at[c], x_recv.at[c])
-
-    pltpu.make_async_copy(g_hbm.at[r], g_in.at[r], g_recv.at[r]).start()
-    for i in range(1, nr):
-        g_copy(i).start()
+            src_ref=src, dst_ref=dst, send_sem=send_sem, recv_sem=recv_sem,
+            device_id=device, device_id_type=MESH)
+
+    def send_early(copy):
+        _, device, src, dst, _, recv_sem = copy
+
+        @pl.when(place_of(device) < place)
+        def _():
+            remote(*copy[1:]).start()
+
+        @pl.when(place_of(device) == place)
+        def _():
+            pltpu.make_async_copy(src, dst, recv_sem).start()
+
+    def send_late(copy, ready):
+        group, device = copy[:2]
+
+        @pl.when(place_of(device) > place)
+        def _():
+            pl.semaphore_wait(ready.at[group], 1)
+            remote(*copy[1:]).start()
+
+    for s in range(nr):
+        tell_earlier(g_ready.at[my_g], (s, c))
+    for j in range(nc):
+        tell_earlier(x_ready.at[my_x], (x_row, j))
+    for i in range(nr):
+        send_early(g_copy(i))
     for i in range(nc):
-        @pl.when(x_stays(i))
-        def _():
-            x_local(i).start()
-
-        @pl.when(jnp.logical_not(x_stays(i)))
-        def _():
-            x_copy(i).start()
+        send_early(x_copy(i))
+    for j in range(nc):
+        tell_earlier(peers, (r, j))
+    for i in range(nr):
+        send_late(g_copy(i), g_ready)
+    for i in range(nc):
+        send_late(x_copy(i), x_ready)
 
     for load in loads:
         load.wait()
@@ -131,7 +173,9 @@
         sources, _, width = arrived.shape
         steps = width // HALF
         for s in range(sources):
-            pltpu.make_async_copy(arrived.at[s], arrived.at[s], recv_sem.at[s]).wait()
+            if s % (sources // 4) == 0:
+                some = arrived.at[pl.ds(s, sources // 4)]
+                pltpu.make_async_copy(some, some, recv_sem.at[4 * s // sources]).wait()
             block = arrived[s].astype(F32)
             for k in range(steps):
                 spread[pl.ds((s * steps + k) * TOK, TOK), :] = block[:, k * HALF:(k + 1) * HALF]
@@ -164,7 +208,12 @@
                 mine = jnp.where(mask, found[t * FP:(t + 1) * FP], 0.0)
                 picked[side, t:t + 1, at] = jnp.sum(mine, axis=0, keepdims=True)
 
+    wait_for(peers, sum((place_of((r, j)) > place).astype(jnp.int32) for j in range(nc)))
+    for i in range(1, nr):
+        signal(everyone, ((r + i) % nr, c))
+
     spectrum(0, g_in, g_recv, rows)
+
     spectrum(1, x_in, x_recv, cols)
 
     def norming(loc_ref):
@@ -175,50 +224,32 @@
     for k in range(nc):
         part[k] = total[:, k * width:(k + 1) * width]
 
-    got_col[c] = part[c]
-
-    def col_copy(i):
-        d = lax.rem(c + i, nc)
-        return pltpu.make_async_remote_copy(
-            src_ref=part.at[d], dst_ref=got_col.at[c], send_sem=c_send.at[i], recv_sem=c_recv.at[c],
-            device_id=(r, d), device_id_type=MESH)
-
-    for i in range(1, nc):
-        col_copy(i).start()
-    for i in range(1, nc):
-        d = lax.rem(c + i, nc)
-        pltpu.make_async_copy(got_col.at[d], got_col.at[d], c_recv.at[d]).wait()
-    mine = got_col[0]
-    for k in range(1, nc):
-        mine = mine + got_col[k]
-    sent_row[...] = mine
-    got_row[r] = mine
-
-    def row_copy(i):
-        d = lax.rem(r + i, nr)
-        return pltpu.make_async_remote_copy(
-            src_ref=sent_row, dst_ref=got_row.at[r], send_sem=r_send.at[i], recv_sem=r_recv.at[r],
-            device_id=(d, c), device_id_type=MESH)
-
-    for i in range(1, nr):
-        row_copy(i).start()
-    for i in range(1, nr):
-        d = lax.rem(r + i, nr)
-        pltpu.make_async_copy(got_row.at[d], got_row.at[d], r_recv.at[d]).wait()
-    result = got_row[0]
-    for k in range(1, nr):
-        result = result + got_row[k]
-    o_ref[...] = result
-
-    for i in range(1, nr):
-        g_copy(i).wait_send()
-        row_copy(i).wait_send()
-    for i in range(1, nc):
-        col_copy(i).wait_send()
-    for i in range(nc):
-        @pl.when(jnp.logical_not(x_stays(i)))
-        def _():
-            x_copy(i).wait_send()
+    pl.semaphore_wait(everyone, nr - 1)
+    mine = c + nc * r
+    pltpu.make_async_copy(part.at[c], got.at[mine], p_recv).start()
+    for i in range(nr):
+        for k in range(nc):
+            if i + k:
+                row, col = (r + i) % nr, (c + k) % nc
+                remote((row, col), part.at[col], got.at[mine], p_send, p_recv).start()
+    pltpu.make_async_copy(got, got, p_recv).wait()
+    o_ref[...] = jnp.sum(got[...], axis=0)
+
+    sent = got.at[pl.ds(0, nr * nc - 1)]
+    pltpu.make_async_copy(sent, sent, p_send).wait()
+
+    def all_sent(copies, source, sem):
+        n = source.shape[0]
+        stays = [(place_of(device) == place).astype(jnp.int32) for _, device, *_ in copies]
+        stays = sum(stays[1:], stays[0])
+        for left in (0, 1):
+            @pl.when(stays == left)
+            def _():
+                moved = source.at[pl.ds(0, n - left)]
+                pltpu.make_async_copy(moved, moved, sem).wait()
+
+    all_sent([g_copy(i) for i in range(nr)], g_hbm, g_send)
+    all_sent([x_copy(i) for i in range(nc)], x_hbm, x_send)
 
 
 def solution(mesh):
@@ -230,7 +261,7 @@
         x = tokens_in.reshape(nc, TOK, tokens_in.shape[1])
         g = out_grads.reshape(nr, TOK, out_grads.shape[1])
         width = locs // nc
-        dma = pltpu.SemaphoreType.DMA
+        dma, regular = pltpu.SemaphoreType.DMA, pltpu.SemaphoreType.REGULAR
         out = pl.pallas_call(
             lambda *refs: kernel(nr, nc, *refs),
             out_shape=jax.ShapeDtypeStruct((1, width), F32),
@@ -252,13 +283,11 @@
                 pltpu.VMEM((2, 2 * HALF, locs), BF16),
                 pltpu.VMEM((2, TOK, locs), F32),
                 pltpu.VMEM((nc, 1, width), F32),
-                pltpu.VMEM((nc, 1, width), F32),
-                pltpu.VMEM((1, width), F32),
-                pltpu.VMEM((nr, 1, width), F32),
-                dma((5,)), dma((nc,)), dma((nc,)), dma((nr,)), dma((nr,)),
-                dma((nc,)), dma((nc,)), dma((nr,)), dma((nr,)),
+                pltpu.VMEM((nr * nc, 1, width), F32),
+                dma((5,)), dma, dma((4,)), dma, dma((4,)), dma, dma,
+                regular((nc,)), regular((nr,)), regular, regular,
             ],
-            compiler_params=pltpu.CompilerParams(collective_id=0, has_side_effects=True, vmem_limit_bytes=48 << 20),
+            compiler_params=pltpu.CompilerParams(collective_id=0, has_side_effects=True),
             name="spectral",
         )(x, g, loc_rows.reshape(1, locs), loc_cols.reshape(1, locs),
           jnp.asarray(first), jnp.asarray(twiddle), jnp.asarray(second))

time: 35.8 us -> 29.8 us (0.83)
  local copies, waits for them, and re-layouts: 6.52 us -> 1.1 us
    unnamed x15 -> x3, local copies, waits for them, and re-layouts: 6.52 us -> 1.1 us
where the time goes in v1:
time: 29.8 us; the launch traced here: 29.7 us
  Pallas kernels  28.6 us (96%)
  local copies, waits for them, and re-layouts  1.1 us (4%)
    pallas_call x1, Pallas kernels, local(): pl.pallas_call(lambda *refs: kernel(nr, nc, *refs), out_shape=jax.ShapeDt...  28.6 us
    unnamed x3, local copies, waits for them, and re-layouts  1.1 us

profile of v1, /device:TPU:1, one launch (start us, length us, event | category | flops | bytes accessed | tf_op | source)
XLA Modules:
  0.0 29.7 jit_solution(962612570479017259)
XLA Ops:
  0.0 28.6 %spectral.1 = f32[1,128]{1,0:T(1,128)} custom-call(bf16[16,8,1024]{2,1,0:T(8,128)(2,1)} %bitcast.5, bf16[8,8,2048]{2,1,0:T(8,128)(2,1)} %bitcast.6, s32[1,2048]{1,0:T(1,128)} %bitcast.7, s32[1,2048]{1,0:T(1,128)} %bitcast.8, bf16[272,256]{1,0:T(8,128)(2,1)} %constant.6.clone.refs_4_, f32[2,136,128]{2,1,0:T(8,128)} %constant.7.clone.refs_5_, ...), custom_call_target="tpu_custom_call" | custom-call | tf_op jit(solution)/shard_map/spectral/pallas_call | solution.py:265
  28.6 0.0 copy-start
  28.6 0.6 %copy-done = f32[1,128]{1,0:T(1,128)S(1)} copy-done((f32[1,128]{1,0:T(1,128)S(1)}, f32[1,128]{1,0:T(1,128)}, u32[]{:S(2)}) %copy-start) | copy-done | bytes 536
  29.2 0.5 %copy.9 = f32[128]{0:T(128)} copy(f32[128]{0:T(128)S(1)} %bitcast.9) | data formatting | bytes 1024
Async XLA Ops:
  28.6 0.6 %copy-start = (f32[1,128]{1,0:T(1,128)S(1)}, f32[1,128]{1,0:T(1,128)}, u32[]{:S(2)}) copy-start(f32[1,128]{1,0:T(1,128)} %spectral.1) | copy-start | bytes 1540

commit v2 on v1

--- a/solution.py
+++ b/solution.py
@@ -51,33 +51,40 @@
 
 
 def kernel(nr, nc, x_hbm, g_hbm, rows_hbm, cols_hbm, first_hbm, twiddle_hbm, second_hbm, o_ref,
-           x_in, g_in, rows, cols, first, twiddle, second, spread, packed, z_high, z_low, d_pair,
+           x_own, g_own, x_in, g_in, rows, cols, first, twiddle, second, spread, packed, z_high, z_low, d_pair,
            pick, picked, part, got,
-           load_sem, x_send, x_recv, g_send, g_recv, p_send, p_recv, x_ready, g_ready, peers, everyone):
+           load_sem, own_sem, x_send, x_recv, g_send, g_recv, p_send, p_recv, x_ready, g_ready, peers, everyone):
     r, c = lax.axis_index("row"), lax.axis_index("col")
-    y, core, z, x = r // 2, r % 2, c // 4, c % 4
+    y, core, z, x = r >> 1, r & 1, c >> 2, c & 3
     locs = rows.shape[1]
 
+    own = [pltpu.make_async_copy(g_hbm, g_own, own_sem.at[0]), pltpu.make_async_copy(x_hbm, x_own, own_sem.at[1])]
+    for load in own:
+        load.start()
+
     def row_place(row):
-        return (4 * (row // 2) - 2 * (row % 2)) * nr * nc + row
+        at = row >> 1
+        return (8 * ((at + 3) >> 2) - ((at + 1) >> 2) - 3 * (row & 1)) * nr * nc + row
 
     def col_place(col):
-        return (6 * (col // 4) + 5 * (col % 4) - 7 * (col % 4 // 3)) * nr * nc + col * nr
+        plane, at = col >> 2, col & 3
+        late = 9 * ((plane + 3) >> 2) + 3 * (plane >> 1) + ((plane + 1) >> 2) + at + ((at + 1) >> 2)
+        return late * nr * nc + col * nr
 
     def place_of(device):
         return row_place(device[0]) + col_place(device[1])
 
     place = place_of((r, c))
 
-    x_row = 2 * z + x // 2
-    my_g = 2 * ((y - z + 4) % 4) + core
-    my_x = nr * (x % 2) + my_g
+    x_row = 2 * z + (x >> 1)
+    my_g = 2 * ((y - z + 4) & 3) + core
+    my_x = nr * (x & 1) + my_g
 
     def x_dest(j):
-        return 2 * ((y + j // 2) % 4) + j % 2, 4 * y + 2 * core + j // nr
+        return 2 * ((y + (j >> 1)) & 3) + (j & 1), 4 * y + 2 * core + (j >> 3)
 
     def g_dest(s):
-        return 2 * ((z + s // 2) % 4) + s % 2, c
+        return 2 * ((z + (s >> 1)) & 3) + (s & 1), c
 
     def signal(sem, device):
         pl.semaphore_signal(sem, inc=1, device_id=device, device_id_type=MESH)
@@ -113,12 +120,12 @@
             signal(sem, device)
 
     def g_copy(i):
-        s = (r + i) % nr
-        return s, g_dest(s), g_hbm.at[s], g_in.at[r], g_send, g_recv.at[y]
+        s = (r + i) & (nr - 1)
+        return s, g_dest(s), g_own.at[s], g_in.at[r], g_send, g_recv.at[y]
 
     def x_copy(i):
-        j = (c + i) % nc
-        return j, x_dest(j), x_hbm.at[j], x_in.at[c], x_send, x_recv.at[z]
+        j = (c + i) & (nc - 1)
+        return j, x_dest(j), x_own.at[j], x_in.at[c], x_send, x_recv.at[z]
 
     def remote(device, src, dst, send_sem, recv_sem):
         return pltpu.make_async_remote_copy(
@@ -148,8 +155,10 @@
         tell_earlier(g_ready.at[my_g], (s, c))
     for j in range(nc):
         tell_earlier(x_ready.at[my_x], (x_row, j))
+    own[0].wait()
     for i in range(nr):
         send_early(g_copy(i))
+    own[1].wait()
     for i in range(nc):
         send_early(x_copy(i))
     for j in range(nc):
@@ -198,19 +207,21 @@
         high = d.astype(BF16)
         d_pair[:, :HALF] = high
         d_pair[:, HALF:] = (d - high.astype(F32)).astype(BF16)
-        tile = 256
+        tile, group = 256, TOK // 2
         for k in range(locs // tile):
             at = slice(k * tile, (k + 1) * tile)
             slot, _ = digits(loc_ref[:, at])
-            found = jnp.dot(d_pair[...], pick[side, :, at], preferred_element_type=F32)
             mask = lax.broadcasted_iota(jnp.int32, (FP, tile), 0) == slot
-            for t in range(TOK):
-                mine = jnp.where(mask, found[t * FP:(t + 1) * FP], 0.0)
-                picked[side, t:t + 1, at] = jnp.sum(mine, axis=0, keepdims=True)
+            for start in range(0, TOK, group):
+                lines = d_pair[start * FP:(start + group) * FP, :]
+                found = jnp.dot(lines, pick[side, :, at], preferred_element_type=F32)
+                for t in range(group):
+                    mine = jnp.where(mask, found[t * FP:(t + 1) * FP], 0.0)
+                    picked[side, start + t:start + t + 1, at] = jnp.sum(mine, axis=0, keepdims=True)
 
     wait_for(peers, sum((place_of((r, j)) > place).astype(jnp.int32) for j in range(nc)))
     for i in range(1, nr):
-        signal(everyone, ((r + i) % nr, c))
+        signal(everyone, ((r + i) & (nr - 1), c))
 
     spectrum(0, g_in, g_recv, rows)
 
@@ -230,7 +241,7 @@
     for i in range(nr):
         for k in range(nc):
             if i + k:
-                row, col = (r + i) % nr, (c + k) % nc
+                row, col = (r + i) & (nr - 1), (c + k) & (nc - 1)
                 remote((row, col), part.at[col], got.at[mine], p_send, p_recv).start()
     pltpu.make_async_copy(got, got, p_recv).wait()
     o_ref[...] = jnp.sum(got[...], axis=0)
@@ -248,8 +259,8 @@
                 moved = source.at[pl.ds(0, n - left)]
                 pltpu.make_async_copy(moved, moved, sem).wait()
 
-    all_sent([g_copy(i) for i in range(nr)], g_hbm, g_send)
-    all_sent([x_copy(i) for i in range(nc)], x_hbm, x_send)
+    all_sent([g_copy(i) for i in range(nr)], g_own, g_send)
+    all_sent([x_copy(i) for i in range(nc)], x_own, x_send)
 
 
 def solution(mesh):
@@ -268,6 +279,8 @@
             in_specs=[pl.BlockSpec(memory_space=pl.ANY)] * 7,
             out_specs=pl.BlockSpec(memory_space=pltpu.VMEM),
             scratch_shapes=[
+                pltpu.VMEM(x.shape, BF16),
+                pltpu.VMEM(g.shape, BF16),
                 pltpu.VMEM((nc, TOK, x.shape[2]), BF16),
                 pltpu.VMEM((nr, TOK, g.shape[2]), BF16),
                 pltpu.VMEM((1, locs), jnp.int32),
@@ -284,7 +297,7 @@
                 pltpu.VMEM((2, TOK, locs), F32),
                 pltpu.VMEM((nc, 1, width), F32),
                 pltpu.VMEM((nr * nc, 1, width), F32),
-                dma((5,)), dma, dma((4,)), dma, dma((4,)), dma, dma,
+                dma((5,)), dma((2,)), dma, dma((4,)), dma, dma((4,)), dma, dma,
                 regular((nc,)), regular((nr,)), regular, regular,
             ],
             compiler_params=pltpu.CompilerParams(collective_id=0, has_side_effects=True),

time: 29.8 us -> 29.4 us (0.987)
  Pallas kernels: 28.6 us -> 28.1 us
    pallas_call x1, Pallas kernels: 28.6 us -> 28.1 us  [local(): pl.pallas_call(lambda *refs: kernel(nr, nc, *refs), out_shape=jax.ShapeDt...]
where the time goes in v2:
time: 29.4 us; the launch traced here: 29.3 us
  Pallas kernels  28.1 us (96%)
  local copies, waits for them, and re-layouts  1.1 us (4%)
    pallas_call x1, Pallas kernels, local(): pl.pallas_call(lambda *refs: kernel(nr, nc, *refs), out_shape=jax.ShapeDt...  28.1 us
    unnamed x3, local copies, waits for them, and re-layouts  1.1 us

profile of v2, /device:TPU:1, one launch (start us, length us, event | category | flops | bytes accessed | tf_op | source)
XLA Modules:
  0.0 29.3 jit_solution(18197034688596237191)
XLA Ops:
  0.0 28.1 %spectral.1 = f32[1,128]{1,0:T(1,128)} custom-call(bf16[16,8,1024]{2,1,0:T(8,128)(2,1)} %bitcast.5, bf16[8,8,2048]{2,1,0:T(8,128)(2,1)} %bitcast.6, s32[1,2048]{1,0:T(1,128)} %bitcast.7, s32[1,2048]{1,0:T(1,128)} %bitcast.8, bf16[272,256]{1,0:T(8,128)(2,1)} %constant.6.clone.refs_4_, f32[2,136,128]{2,1,0:T(8,128)} %constant.7.clone.refs_5_, ...), custom_call_target="tpu_custom_call" | custom-call | tf_op jit(solution)/shard_map/spectral/pallas_call | solution.py:276
  28.2 0.0 copy-start
  28.2 0.6 %copy-done = f32[1,128]{1,0:T(1,128)S(1)} copy-done((f32[1,128]{1,0:T(1,128)S(1)}, f32[1,128]{1,0:T(1,128)}, u32[]{:S(2)}) %copy-start) | copy-done | bytes 536
  28.7 0.5 %copy.9 = f32[128]{0:T(128)} copy(f32[128]{0:T(128)S(1)} %bitcast.9) | data formatting | bytes 1024
Async XLA Ops:
  28.2 0.6 %copy-start = (f32[1,128]{1,0:T(1,128)S(1)}, f32[1,128]{1,0:T(1,128)}, u32[]{:S(2)}) copy-start(f32[1,128]{1,0:T(1,128)} %spectral.1) | copy-start | bytes 1540

commit v3 on v2

--- a/solution.py
+++ b/solution.py
@@ -124,7 +124,7 @@
         return s, g_dest(s), g_own.at[s], g_in.at[r], g_send, g_recv.at[y]
 
     def x_copy(i):
-        j = (c + i) & (nc - 1)
+        j = (c - i) & (nc - 1)
         return j, x_dest(j), x_own.at[j], x_in.at[c], x_send, x_recv.at[z]
 
     def remote(device, src, dst, send_sem, recv_sem):
@@ -238,8 +238,8 @@
     pl.semaphore_wait(everyone, nr - 1)
     mine = c + nc * r
     pltpu.make_async_copy(part.at[c], got.at[mine], p_recv).start()
-    for i in range(nr):
-        for k in range(nc):
+    for k in range(nc):
+        for i in range(nr):
             if i + k:
                 row, col = (r + i) & (nr - 1), (c + k) & (nc - 1)
                 remote((row, col), part.at[col], got.at[mine], p_send, p_recv).start()

time: 29.4 us -> 28.7 us (0.976)
  Pallas kernels: 28.1 us -> 27.5 us
    pallas_call x1, Pallas kernels: 28.1 us -> 27.5 us  [local(): pl.pallas_call(lambda *refs: kernel(nr, nc, *refs), out_shape=jax.ShapeDt...]
where the time goes in v3:
time: 28.7 us; the launch traced here: 28.6 us
  Pallas kernels  27.5 us (96%)
  local copies, waits for them, and re-layouts  1.1 us (4%)
    pallas_call x1, Pallas kernels, local(): pl.pallas_call(lambda *refs: kernel(nr, nc, *refs), out_shape=jax.ShapeDt...  27.5 us
    unnamed x3, local copies, waits for them, and re-layouts  1.1 us

profile of v3, /device:TPU:1, one launch (start us, length us, event | category | flops | bytes accessed | tf_op | source)
XLA Modules:
  0.0 28.6 jit_solution(15547764556081888093)
XLA Ops:
  0.0 27.5 %spectral.1 = f32[1,128]{1,0:T(1,128)} custom-call(bf16[16,8,1024]{2,1,0:T(8,128)(2,1)} %bitcast.5, bf16[8,8,2048]{2,1,0:T(8,128)(2,1)} %bitcast.6, s32[1,2048]{1,0:T(1,128)} %bitcast.7, s32[1,2048]{1,0:T(1,128)} %bitcast.8, bf16[272,256]{1,0:T(8,128)(2,1)} %constant.6.clone.refs_4_, f32[2,136,128]{2,1,0:T(8,128)} %constant.7.clone.refs_5_, ...), custom_call_target="tpu_custom_call" | custom-call | tf_op jit(solution)/shard_map/spectral/pallas_call | solution.py:276
  27.5 0.0 copy-start
  27.5 0.6 %copy-done = f32[1,128]{1,0:T(1,128)S(1)} copy-done((f32[1,128]{1,0:T(1,128)S(1)}, f32[1,128]{1,0:T(1,128)}, u32[]{:S(2)}) %copy-start) | copy-done | bytes 536
  28.1 0.5 %copy.9 = f32[128]{0:T(128)} copy(f32[128]{0:T(128)S(1)} %bitcast.9) | data formatting | bytes 1024
Async XLA Ops:
  27.5 0.6 %copy-start = (f32[1,128]{1,0:T(1,128)S(1)}, f32[1,128]{1,0:T(1,128)}, u32[]{:S(2)}) copy-start(f32[1,128]{1,0:T(1,128)} %spectral.1) | copy-start | bytes 1540
